TPU v7x, 32 devices: a whole 2x2x4 slice. The times are simulated.
32 devices in a mesh: rows: 16 (over z, y, core), heads: 2 (over x).
Axes of the slice: x: 2, y: 2, z: 4, core: 2. Of those that a mesh axis runs over, the one named last changes fastest.
Arguments:
- tokens: bfloat16 [32768, 768], P(('rows', 'heads')), may hold values from -6 to 6
- crop_lengths: int32 [16], P('rows'), may hold values from 1025 to 2048, as said below
- lead_index: int32 [16], P('rows'), may hold values from 0 to 31
- valid_mask: int32 [32768], P(('rows', 'heads')), may hold values from 0 to 1, as said below
- lead_table: float32 [32, 768], replicated, may hold values from -3 to 3
- ln1_gain: float32 [768], replicated, may hold values from 0.25 to 1.75
- ln1_shift: float32 [768], replicated, may hold values from -1.5 to 1.5
- w_query: bfloat16 [768, 768], P(None, 'heads'), may hold values from -0.3125 to 0.3125
- w_key: bfloat16 [768, 768], P(None, 'heads'), may hold values from -0.3125 to 0.3125
- w_value: bfloat16 [768, 768], P(None, 'heads'), may hold values from -0.21875 to 0.21875
- b_query: bfloat16 [768], P('heads'), may hold values from -1.5 to 1.5
- b_value: bfloat16 [768], P('heads'), may hold values from -1.5 to 1.5
- w_out: bfloat16 [768, 768], P('heads'), may hold values from -1.75 to 1.75
- b_out: float32 [768], replicated, may hold values from -1.5 to 1.5
- ln2_gain: float32 [768], replicated, may hold values from 0.25 to 1.75
- ln2_shift: float32 [768], replicated, may hold values from -1.5 to 1.5
- w_up: bfloat16 [768, 3072], P(None, 'heads'), may hold values from -0.21875 to 0.21875
- b_up: bfloat16 [3072], P('heads'), may hold values from -1.5 to 1.5
- w_down: bfloat16 [3072, 768], P('heads'), may hold values from -0.109375 to 0.109375
- b_down: float32 [768], replicated, may hold values from -1.5 to 1.5
- w_gater: float32 [768, 3], replicated, may hold values from -0.3125 to 0.3125
- cotangent: bfloat16 [32768, 768], P(('rows', 'heads')), may hold values from -6 to 6
Outputs:
- block_out: bfloat16 [32768, 768], P(('rows', 'heads'))
- penalty: float32 [], replicated
- grad_tokens: float32 [32768, 768], P(('rows', 'heads'))
- grad_lead_table: float32 [32, 768], replicated
- grad_ln1_gain: float32 [768], replicated
- grad_ln1_shift: float32 [768], replicated
- grad_query: float32 [768, 768], P('rows', 'heads')
- grad_key: float32 [768, 768], P('rows', 'heads')
- grad_value: float32 [768, 768], P('rows', 'heads')
- grad_b_query: float32 [768], P('heads')
- grad_b_value: float32 [768], P('heads')
- grad_out: float32 [768, 768], P('heads', 'rows')
- grad_b_out: float32 [768], replicated
- grad_ln2_gain: float32 [768], replicated
- grad_ln2_shift: float32 [768], replicated
- grad_up: float32 [768, 3072], P('rows', 'heads')
- grad_b_up: float32 [3072], P('heads')
- grad_down: float32 [3072, 768], P('heads', 'rows')
- grad_b_down: float32 [768], replicated
- grad_gater: float32 [768, 3], replicated
Inputs may be any that keep to these rules, and one draw needn't show every extreme that they name: `crop_lengths`: every crop uses more than half of its 2048 slots, and some crop uses all of them. `valid_mask`: the first pixel of every crop counts.
All inputs are finite; a program needn't handle non-finite values.
Results may differ from a plain program's by a relative error of at most 0.014.
The roundings to bfloat16 on the way count: a program that leaves them out, or rounds other values in their place, can miss the bound.
Values may be sent and summed in bfloat16 or wider, within the bound.
No kernel may reach another device: no remote copies, remote signals or barrier semaphores. Data moves between devices by JAX's collectives and lax.ppermute only.
A program may use at most 320 MiB of HBM per device.

v0:
```python
import jax
import jax.numpy as jnp
from jax import lax
from jax.sharding import PartitionSpec as P

HEAD_DIM = 64


entropy_weight = 16.0


def layer_norm(values, gain, shift):
    centre = values - jnp.mean(values, axis=-1, keepdims=True)
    spread = jnp.mean(centre * centre, axis=-1, keepdims=True)
    return centre * lax.rsqrt(spread + 1e-05) * gain + shift


def gelu_exact(values):
    return jax.nn.gelu(values, approximate=False)


def outer_rows(left, right):
    return lax.dot_general(
        left, right, (((0,), (0,)), ((), ())), preferred_element_type=jnp.float32
    )


def times_transposed(left, right):
    return lax.dot_general(
        left, right, (((1,), (1,)), ((), ())), preferred_element_type=jnp.float32
    )


def per_device(
    tokens,
    crop_lengths,
    lead_index,
    valid_mask,
    lead_table,
    ln1_gain,
    ln1_shift,
    w_query,
    w_key,
    w_value,
    b_query,
    b_value,
    w_out,
    b_out,
    ln2_gain,
    ln2_shift,
    w_up,
    b_up,
    w_down,
    b_down,
    w_gater,
    cotangent,
):
    f32 = jnp.float32
    bf16 = jnp.bfloat16
    own_rows = tokens.shape[0]
    head_index = lax.axis_index("heads")
    length = crop_lengths[0]
    picked = jnp.arange(lead_table.shape[0], dtype=jnp.int32) == lead_index[0]
    embedding = jnp.sum(jnp.where(picked[:, None], lead_table, 0.0), axis=0)
    x_zero = tokens.astype(f32) + embedding
    normed_one = layer_norm(x_zero, ln1_gain, ln1_shift).astype(bf16)
    full_normed = lax.all_gather(normed_one, "heads", axis=0, tiled=True)
    crop_rows = full_normed.shape[0]
    local_heads = w_query.shape[1] // HEAD_DIM
    query = (
        jnp.dot(full_normed, w_query, preferred_element_type=f32) + b_query.astype(f32)
    ).astype(bf16)
    key_proj = jnp.dot(full_normed, w_key, preferred_element_type=f32).astype(bf16)
    value = (
        jnp.dot(full_normed, w_value, preferred_element_type=f32) + b_value.astype(f32)
    ).astype(bf16)
    query3 = query.reshape(crop_rows, local_heads, HEAD_DIM)
    key3 = key_proj.reshape(crop_rows, local_heads, HEAD_DIM)
    value3 = value.reshape(crop_rows, local_heads, HEAD_DIM)
    key_ok = jnp.arange(crop_rows, dtype=jnp.int32) < length
    block_rows = min(512, crop_rows)
    score_scale = HEAD_DIM ** (-0.5)

    def scores_of(start):
        query_block = lax.slice_in_dim(query3, start, start + block_rows, axis=0)
        scores = (
            jnp.einsum("qhd,khd->hqk", query_block, key3, preferred_element_type=f32) * score_scale
        )
        return (query_block, jnp.where(key_ok[None, None, :], scores, -1e30))

    mixed_blocks = []
    log_totals = []
    for block in range(crop_rows // block_rows):
        start = block * block_rows
        query_block, scores = scores_of(start)
        probs = jax.nn.softmax(scores, axis=-1)
        log_totals.append(jax.nn.logsumexp(scores, axis=-1))
        mixed = jnp.einsum("hqk,khd->qhd", probs.astype(bf16), value3, preferred_element_type=f32)
        mixed_blocks.append(mixed.astype(bf16))
    attn_heads = jnp.concatenate(mixed_blocks, axis=0).reshape(crop_rows, local_heads * HEAD_DIM)
    attn_sum = lax.psum_scatter(
        jnp.dot(attn_heads, w_out, preferred_element_type=f32),
        "heads",
        scatter_dimension=0,
        tiled=True,
    )
    hidden_one = x_zero + (attn_sum + b_out)
    normed_two = layer_norm(hidden_one, ln2_gain, ln2_shift).astype(bf16)
    mlp_rows = lax.all_gather(normed_two, "heads", axis=0, tiled=True)
    up_full, down_full, bias_full = (w_up, w_down, b_up)
    pre_act = jnp.dot(mlp_rows, up_full, preferred_element_type=f32) + bias_full.astype(f32)
    activation = gelu_exact(pre_act).astype(bf16)
    branch = lax.psum_scatter(
        jnp.dot(activation, w_down, preferred_element_type=f32).astype(jnp.bfloat16),
        "heads",
        scatter_dimension=0,
        tiled=True,
    ).astype(jnp.float32)
    output = hidden_one + (branch + b_down)
    logits = jnp.einsum("dc,td->ct", w_gater, output, precision=lax.Precision.HIGHEST)
    log_probs = jax.nn.log_softmax(logits, axis=0)
    gate_probs = jnp.exp(log_probs)
    entropy = -jnp.sum(gate_probs * log_probs, axis=0)
    positions = head_index * own_rows + jnp.arange(own_rows, dtype=jnp.int32)
    counted = ((positions < length) & (valid_mask == 1)).astype(f32)
    entropy_total, count_total = lax.psum(
        (jnp.sum(counted * entropy), jnp.sum(counted)), ("rows", "heads")
    )
    penalty = entropy_total / count_total
    mean_logit = jnp.sum(gate_probs * logits, axis=0)
    d_logits = entropy_weight / count_total * counted * (-gate_probs * (logits - mean_logit))
    d_output = cotangent.astype(f32) + jnp.einsum(
        "dc,ct->td", w_gater, d_logits, precision=lax.Precision.HIGHEST
    )
    d_gater = jnp.einsum("td,ct->dc", output, d_logits, precision=lax.Precision.HIGHEST)
    d_branch = d_output.astype(bf16)
    d_bias_down = jnp.sum(d_branch.astype(f32), axis=0)
    unused, gelu_back = jax.vjp(gelu_exact, pre_act)
    branch_rows = lax.all_gather(d_branch, "heads", axis=0, tiled=True)
    d_down = outer_rows(activation, branch_rows)
    d_pre = gelu_back(times_transposed(branch_rows, w_down))[0].astype(bf16)
    d_up = outer_rows(mlp_rows, d_pre)
    d_bias_up = jnp.sum(d_pre.astype(f32), axis=0)
    d_normed_two = lax.psum_scatter(
        times_transposed(d_pre, w_up).astype(jnp.bfloat16), "heads", scatter_dimension=0, tiled=True
    ).astype(jnp.float32)
    unused_two, norm_two_back = jax.vjp(layer_norm, hidden_one, ln2_gain, ln2_shift)
    d_hidden_norm, d_gain_two, d_shift_two = norm_two_back(d_normed_two)
    d_hidden = d_output + d_hidden_norm
    d_attn = d_hidden.astype(bf16)
    d_bias_out = jnp.sum(d_attn.astype(f32), axis=0)
    attn_rows = lax.all_gather(d_attn, "heads", axis=0, tiled=True)
    d_w_out = outer_rows(attn_heads, attn_rows)
    d_heads = (
        times_transposed(attn_rows, w_out).astype(bf16).reshape(crop_rows, local_heads, HEAD_DIM)
    )
    d_query_blocks = []
    d_key_sum = jnp.zeros((crop_rows, local_heads, HEAD_DIM), f32)
    d_value_sum = jnp.zeros((crop_rows, local_heads, HEAD_DIM), f32)
    for block in range(crop_rows // block_rows):
        start = block * block_rows
        query_block, scores = scores_of(start)
        probs = jnp.exp(scores - log_totals[block][..., None])
        grad_block = lax.slice_in_dim(d_heads, start, start + block_rows, axis=0)
        d_probs = jnp.einsum("qhd,khd->hqk", grad_block, value3, preferred_element_type=f32)
        row_dot = jnp.sum(probs * d_probs, axis=-1, keepdims=True)
        d_scores = (probs * (d_probs - row_dot)).astype(bf16)
        d_query_blocks.append(
            jnp.einsum("hqk,khd->qhd", d_scores, key3, preferred_element_type=f32) * score_scale
        )
        d_key_sum = (
            d_key_sum
            + jnp.einsum("hqk,qhd->khd", d_scores, query_block, preferred_element_type=f32)
            * score_scale
        )
        d_value_sum = d_value_sum + jnp.einsum(
            "hqk,qhd->khd", probs.astype(bf16), grad_block, preferred_element_type=f32
        )
    local_width = local_heads * HEAD_DIM
    d_query = jnp.concatenate(d_query_blocks, axis=0).reshape(crop_rows, local_width).astype(bf16)
    d_key = d_key_sum.reshape(crop_rows, local_width).astype(bf16)
    d_value = d_value_sum.reshape(crop_rows, local_width).astype(bf16)
    d_bias_query = jnp.sum(d_query.astype(f32), axis=0)
    d_bias_value = jnp.sum(d_value.astype(f32), axis=0)
    d_w_query = outer_rows(full_normed, d_query)
    d_w_key = outer_rows(full_normed, d_key)
    d_w_value = outer_rows(full_normed, d_value)
    total = times_transposed(d_query, w_query)
    total = total + times_transposed(d_key, w_key)
    d_normed_one = lax.psum_scatter(
        (total + times_transposed(d_value, w_value)).astype(jnp.bfloat16),
        "heads",
        scatter_dimension=0,
        tiled=True,
    ).astype(jnp.float32)
    unused_one, norm_one_back = jax.vjp(layer_norm, x_zero, ln1_gain, ln1_shift)
    d_input_norm, d_gain_one, d_shift_one = norm_one_back(d_normed_one)
    d_tokens = d_hidden + d_input_norm
    d_table = jnp.where(picked[:, None], jnp.sum(d_tokens, axis=0)[None, :], 0.0)
    d_w_query, d_w_key, d_w_value, d_w_out, d_up, d_down = (
        lax.psum_scatter(d_w_query, "rows", scatter_dimension=0, tiled=True),
        lax.psum_scatter(d_w_key, "rows", scatter_dimension=0, tiled=True),
        lax.psum_scatter(d_w_value, "rows", scatter_dimension=0, tiled=True),
        lax.psum_scatter(d_w_out, "rows", scatter_dimension=1, tiled=True),
        lax.psum_scatter(d_up, "rows", scatter_dimension=0, tiled=True),
        lax.psum_scatter(d_down, "rows", scatter_dimension=1, tiled=True),
    )
    d_bias_query, d_bias_value, d_bias_up = lax.psum(
        (d_bias_query, d_bias_value, d_bias_up), "rows"
    )
    d_table, d_gain_one, d_shift_one, d_gain_two, d_shift_two, d_bias_out, d_bias_down, d_gater = (
        lax.psum(
            (
                d_table,
                d_gain_one,
                d_shift_one,
                d_gain_two,
                d_shift_two,
                d_bias_out,
                d_bias_down,
                d_gater,
            ),
            ("rows", "heads"),
        )
    )
    return (
        output.astype(bf16),
        penalty,
        d_tokens,
        d_table,
        d_gain_one,
        d_shift_one,
        d_w_query,
        d_w_key,
        d_w_value,
        d_bias_query,
        d_bias_value,
        d_w_out,
        d_bias_out,
        d_gain_two,
        d_shift_two,
        d_up,
        d_bias_up,
        d_down,
        d_bias_down,
        d_gater,
    )


def solution(mesh):
    in_specs = (
        P(("rows", "heads"), None),
        P("rows"),
        P("rows"),
        P(("rows", "heads")),
        P(),
        P(),
        P(),
        P(None, "heads"),
        P(None, "heads"),
        P(None, "heads"),
        P("heads"),
        P("heads"),
        P("heads", None),
        P(),
        P(),
        P(),
        P(None, "heads"),
        P("heads"),
        P("heads", None),
        P(),
        P(),
        P(("rows", "heads"), None),
    )
    out_specs = (
        P(("rows", "heads"), None),
        P(),
        P(("rows", "heads"), None),
        P(),
        P(),
        P(),
        P("rows", "heads"),
        P("rows", "heads"),
        P("rows", "heads"),
        P("heads"),
        P("heads"),
        P("heads", "rows"),
        P(),
        P(),
        P(),
        P("rows", "heads"),
        P("heads"),
        P("heads", "rows"),
        P(),
        P(),
    )
    return jax.shard_map(
        per_device, mesh=mesh, in_specs=in_specs, out_specs=out_specs, check_vma=False
    )
```

profile of v0, /device:TPU:8, one launch (start us, length us, event | category | flops | bytes accessed | tf_op | source)
XLA Modules:
  0.0 1535.3 jit_solution(198313688964825779)
XLA Ops:
  17.4 45.5 %all-gather.5.cloned.1.call-done = bf16[2048,768]{1,0:T(8,128)(2,1)} async-done(((bf16[1024,768]{1,0:T(8,128)(2,1)}), bf16[2048,768]{1,0:T(8,128)(2,1)}) %all-gather.5.cloned.1.call-update) | async-done | bytes 3145744 | tf_op jit(solution)/shard_map/all_gather | solution.py:67
  211.4 77.2 %reduce-scatter.11.cloned.1.call-done = f32[1024,768]{1,0:T(8,128)} async-done(((f32[2048,768]{1,0:T(8,128)}), f32[1024,768]{1,0:T(8,128)}) %reduce-scatter.11.cloned.1.call-update) | async-done | bytes 3145744 | tf_op jit(solution)/shard_map/reduce_scatter | solution.py:101
  295.6 45.0 %all-gather.7.cloned.1.call-done = bf16[2048,768]{1,0:T(8,128)(2,1)} async-done(((bf16[1024,768]{1,0:T(8,128)(2,1)}), bf16[2048,768]{1,0:T(8,128)(2,1)}) %all-gather.7.cloned.1.call-update) | async-done | bytes 3145744 | tf_op jit(solution)/shard_map/all_gather | solution.py:109
  340.7 33.9 %multiply_convert_fusion.4 = (bf16[2048,1536]{1,0:T(8,128)(2,1)S(1)}, f32[2048,1536]{1,0:T(8,128)}, f32[2048,1536]{1,0:T(8,128)}) fusion(f32[1536]{0:T(1024)S(1)} %convert_element_type.188, bf16[2048,768]{1,0:T(8,128)(2,1)} %all-gather.7.cloned.1.call-done, bf16[768,1536]{1,0:T(8,128)(2,1)S(1)} %copy-done), kind=kOutput, calls=%fused_computation.48 | convolution fusion | flops 5039456256 | bytes 36968448 | tf_op jit(solution)/shard_map/dot_general | solution.py:111
  384.0 43.0 %reduce-scatter.13.cloned.1.call-done = bf16[1024,768]{1,0:T(8,128)(2,1)} async-done(((bf16[2048,768]{1,0:T(8,128)(2,1)}), bf16[1024,768]{1,0:T(8,128)(2,1)}) %reduce-scatter.13.cloned.1.call-update) | async-done | bytes 1572880 | tf_op jit(solution)/shard_map/reduce_scatter | solution.py:113
  433.2 39.5 %psum.92 = f32[]{:T(128)} all-reduce(f32[]{:T(128)} %get-tuple-element.37), channel_id=1, replica_groups=mesh['rows'=16,'heads'=2] {'rows','heads'}, use_global_device_ids=true, to_apply=%region_21.22 | all-reduce | flops 1 | bytes 8 | tf_op jit(solution)/shard_map/psum | solution.py:126
  479.8 46.0 %all-gather.9.cloned.1.call-done = bf16[2048,768]{1,0:T(8,128)(2,1)} async-done(((bf16[1024,768]{1,0:T(8,128)(2,1)}), bf16[2048,768]{1,0:T(8,128)(2,1)}) %all-gather.9.cloned.1.call-update) | async-done | bytes 3145744 | tf_op jit(solution)/shard_map/all_gather | solution.py:139
  525.8 17.5 %convert_reduce_fusion = (f32[1536]{0:T(1024)}, bf16[2048,1536]{1,0:T(8,128)(2,1)S(1)}) fusion(f32[2048,1536]{1,0:T(8,128)} %get-tuple-element.62, bf16[2048,768]{1,0:T(8,128)(2,1)} %all-gather.9.cloned.1.call-done, bf16[1536,768]{1,0:T(8,128)(2,1)} %param.40, f32[2048,1536]{1,0:T(8,128)} %get-tuple-element.82, f32[1536]{0:T(1024)S(1)} %convert_element_type.188), kind=kOutput, calls=%fused_computation.42 | convolution fusion | flops 4885314048 | bytes 36974592 | tf_op jit(solution)/shard_map/dot_general | solution.py:29
  552.5 43.4 %reduce-scatter.15.cloned.1.call-done = bf16[1024,768]{1,0:T(8,128)(2,1)} async-done(((bf16[2048,768]{1,0:T(8,128)(2,1)}), bf16[1024,768]{1,0:T(8,128)(2,1)}) %reduce-scatter.15.cloned.1.call-update) | async-done | bytes 1572880 | tf_op jit(solution)/shard_map/reduce_scatter | solution.py:144
  607.1 44.9 %all-gather.11.cloned.1.call-done = bf16[2048,768]{1,0:T(8,128)(2,1)} async-done(((bf16[1024,768]{1,0:T(8,128)(2,1)}), bf16[2048,768]{1,0:T(8,128)(2,1)}) %all-gather.11.cloned.1.call-update) | async-done | bytes 3145744 | tf_op jit(solution)/shard_map/all_gather | solution.py:152
  656.9 19.7 %multiply_reduce_fusion.3 = (f32[6,512]{1,0:T(8,128)S(1)}, f32[6,512,2048]{2,1,0:T(8,128)}) fusion(f32[6,512,2048]{2,1,0:T(8,128)} %get-tuple-element.81, f32[6,512]{1,0:T(8,128)S(1)} %log_add_fusion.3, bf16[512,6,64]{0,2,1:T(8,128)(2,1)S(1)} %bitcast.170, bf16[2048,6,64]{0,2,1:T(8,128)(2,1)S(1)} %bitcast.153), kind=kOutput, calls=%fused_computation.13 | convolution fusion | flops 824177664 | bytes 52322304 | tf_op jit(solution)/shard_map/qhd,khd->hqk/dot_general | solution.py:165
  676.6 21.6 %multiply_convert_fusion.3 = bf16[6,512,2048]{2,1,0:T(8,128)(2,1)} fusion(f32[6,512,2048]{2,1,0:T(8,128)} %get-tuple-element.93, f32[6,512,2048]{2,1,0:T(8,128)} %get-tuple-element.81, f32[6,512]{1,0:T(8,128)S(1)} %get-tuple-element.92, f32[6,512]{1,0:T(8,128)S(1)} %log_add_fusion.3), kind=kLoop, calls=%fused_computation.12 | loop fusion | flops 25165824 | bytes 62939136 | tf_op jit(solution)/shard_map/convert_element_type | solution.py:167
  728.1 16.1 %multiply_reduce_fusion.2 = (f32[6,512]{1,0:T(8,128)S(1)}, f32[6,512,2048]{2,1,0:T(8,128)}) fusion(f32[6,512,2048]{2,1,0:T(8,128)} %get-tuple-element.79, f32[6,512]{1,0:T(8,128)S(1)} %log_add_fusion.2, bf16[512,6,64]{0,2,1:T(8,128)(2,1)S(1)} %bitcast.177, bf16[2048,6,64]{0,2,1:T(8,128)(2,1)} %bitcast.150), kind=kOutput, calls=%fused_computation.9 | convolution fusion | flops 824177664 | bytes 52322304 | tf_op jit(solution)/shard_map/qhd,khd->hqk/dot_general | solution.py:165
  744.2 21.6 %multiply_convert_fusion.2 = bf16[6,512,2048]{2,1,0:T(8,128)(2,1)} fusion(f32[6,512,2048]{2,1,0:T(8,128)} %get-tuple-element.91, f32[6,512,2048]{2,1,0:T(8,128)} %get-tuple-element.79, f32[6,512]{1,0:T(8,128)S(1)} %get-tuple-element.90, f32[6,512]{1,0:T(8,128)S(1)} %log_add_fusion.2), kind=kLoop, calls=%fused_computation.8 | loop fusion | flops 25165824 | bytes 62939136 | tf_op jit(solution)/shard_map/convert_element_type | solution.py:167
  811.0 21.8 %multiply_convert_fusion.1 = bf16[6,512,2048]{2,1,0:T(8,128)(2,1)} fusion(f32[6,512,2048]{2,1,0:T(8,128)} %get-tuple-element.89, f32[6,512,2048]{2,1,0:T(8,128)} %get-tuple-element.77, f32[6,512]{1,0:T(8,128)S(1)} %get-tuple-element.88, f32[6,512]{1,0:T(8,128)S(1)} %log_add_fusion.1), kind=kLoop, calls=%fused_computation.4 | loop fusion | flops 25165824 | bytes 62939136 | tf_op jit(solution)/shard_map/convert_element_type | solution.py:167
  878.0 21.7 %multiply_convert_fusion = bf16[6,512,2048]{2,1,0:T(8,128)(2,1)} fusion(f32[6,512,2048]{2,1,0:T(8,128)} %get-tuple-element.87, f32[6,512,2048]{2,1,0:T(8,128)} %get-tuple-element.75, f32[6,512]{1,0:T(8,128)S(1)} %get-tuple-element.86, f32[6,512]{1,0:T(8,128)S(1)} %log_add_fusion), kind=kLoop, calls=%fused_computation | loop fusion | flops 25165824 | bytes 62939136 | tf_op jit(solution)/shard_map/convert_element_type | solution.py:167
  1009.8 54.1 %all-reduce.1 = (f32[384]{0:T(512)}, f32[384]{0:T(512)}, f32[1536]{0:T(1024)}) all-reduce(f32[384]{0:T(512)S(1)} %reduce_sum.407, f32[384]{0:T(512)S(1)} %reduce_sum.409, f32[1536]{0:T(1024)S(1)} %copy-done.92), channel_id=1, replica_groups=mesh['rows'=16,'heads'=2] {'rows'}, use_global_device_ids=true, to_apply=%region_47.48 | all-reduce | flops 2304 | bytes 18432 | tf_op jit(solution)/shard_map/psum | solution.py:208
  1064.0 47.5 %all-reduce = (f32[]{:T(128)}, f32[768]{0:T(1024)}, f32[768]{0:T(1024)}, f32[768]{0:T(1024)}, f32[768]{0:T(1024)}, /*index=5*/f32[768]{0:T(1024)}, f32[768]{0:T(1024)}, f32[768,3]{0,1:T(4,128)}) all-reduce(f32[]{:T(128)} %get-tuple-element.38, f32[768]{0:T(1024)S(1)} %get-tuple-element.30, ...), channel_id=1, replica_groups=mesh['rows'=16,'heads'=2] {'rows','heads'}, use_global_device_ids=true, to_apply=%region_19.20 | all-reduce | flops 6913 | bytes 55304 | tf_op jit(solution)/shard_map/psum | solution.py:126
  1112.8 39.9 %reduce-scatter.27.cloned.1.call-done = f32[48,1536]{1,0:T(8,128)} async-done(((f32[768,1536]{1,0:T(8,128)}), f32[48,1536]{1,0:T(8,128)}) %reduce-scatter.27.cloned.1.call-update) | async-done | bytes 294928 | tf_op jit(solution)/shard_map/reduce_scatter | solution.py:205
  1152.8 61.9 %reduce-scatter.25.cloned.1.call-done = f32[384,48]{0,1:T(8,128)} async-done(((f32[384,768]{0,1:T(8,128)}), f32[384,48]{0,1:T(8,128)}) %reduce-scatter.25.cloned.1.call-update) | async-done | bytes 73744 | tf_op jit(solution)/shard_map/reduce_scatter | solution.py:204
  1214.6 61.2 %reduce-scatter.23.cloned.1.call-done = f32[48,384]{1,0:T(8,128)} async-done(((f32[768,384]{1,0:T(8,128)}), f32[48,384]{1,0:T(8,128)}) %reduce-scatter.23.cloned.1.call-update) | async-done | bytes 73744 | tf_op jit(solution)/shard_map/reduce_scatter | solution.py:203
  1275.8 61.3 %reduce-scatter.21.cloned.1.call-done = f32[48,384]{1,0:T(8,128)} async-done(((f32[768,384]{1,0:T(8,128)}), f32[48,384]{1,0:T(8,128)}) %reduce-scatter.21.cloned.1.call-update) | async-done | bytes 73744 | tf_op jit(solution)/shard_map/reduce_scatter | solution.py:202
  1337.1 61.1 %reduce-scatter.19.cloned.1.call-done = f32[48,384]{1,0:T(8,128)} async-done(((f32[768,384]{1,0:T(8,128)}), f32[48,384]{1,0:T(8,128)}) %reduce-scatter.19.cloned.1.call-update) | async-done | bytes 73744 | tf_op jit(solution)/shard_map/reduce_scatter | solution.py:201
  1398.2 127.5 %all-reduce.4.cloned.1.call-done = f32[32,768]{1,0:T(8,128)} async-done(((f32[32,768]{1,0:T(8,128)}), f32[32,768]{1,0:T(8,128)}) %all-reduce.4.cloned.1.call-update) | async-done | bytes 98320 | tf_op jit(solution)/shard_map/psum | solution.py:212
  (336 shorter events, 442.0 us)
Async XLA Ops:
  7.2 333.5 %copy-start = (bf16[768,1536]{1,0:T(8,128)(2,1)S(1)}, bf16[768,1536]{1,0:T(8,128)(2,1)}, u32[]{:S(2)}) copy-start(bf16[768,1536]{1,0:T(8,128)(2,1)} %param.38) | copy-start | bytes 7077892
  7.2 55.7 %all-gather.5.cloned.1.call-start = ((), (), s32[]{:S(2)}) async-start(), calls=%async_computation.10 | async-start | bytes 4718592 | tf_op jit(solution)/shard_map/all_gather | solution.py:67
  16.7 271.9 %reduce-scatter.11.cloned.1.call-start = ((), (), s32[]{:S(2)}) async-start(), calls=%async_computation.11 | async-start | bytes 9437184 | tf_op jit(solution)/shard_map/reduce_scatter | solution.py:101
  67.5 71.0 %copy-start.25 = (bf16[512,384]{0,1:T(8,128)(2,1)}, bf16[512,384]{0,1:T(8,128)(2,1)S(1)}, u32[]{:S(2)}) copy-start(bf16[512,384]{0,1:T(8,128)(2,1)S(1)} %get-tuple-element.73) | copy-start | bytes 1179652
  67.5 104.5 %copy-start.27 = (bf16[512,384]{0,1:T(8,128)(2,1)}, bf16[512,384]{0,1:T(8,128)(2,1)S(1)}, u32[]{:S(2)}) copy-start(bf16[512,384]{0,1:T(8,128)(2,1)S(1)} %get-tuple-element.70) | copy-start | bytes 1179652
  68.9 103.1 %copy-start.3 = (bf16[2048,384]{0,1:T(8,128)(2,1)}, bf16[2048,384]{0,1:T(8,128)(2,1)S(1)}, u32[]{:S(2)}) copy-start(bf16[2048,384]{0,1:T(8,128)(2,1)S(1)} %convolution_convert_fusion.3) | copy-start | bytes 4718596
  103.7 91.2 %copy-start.11 = (bf16[2048,384]{0,1:T(8,128)(2,1)}, bf16[2048,384]{0,1:T(8,128)(2,1)S(1)}, u32[]{:S(2)}) copy-start(bf16[2048,384]{0,1:T(8,128)(2,1)S(1)} %add_convert_fusion.5) | copy-start | bytes 4718596
  211.3 77.2 %copy-start.43 = (f32[768]{0:T(1024)S(1)}, f32[768]{0:T(1024)}, u32[]{:S(2)}) copy-start(f32[768]{0:T(1024)} %copy-done.42) | copy-start | bytes 9220
  211.3 77.2 %copy-start.94 = (f32[768]{0:T(1024)S(1)}, f32[768]{0:T(1024)}, u32[]{:S(2)}) copy-start(f32[768]{0:T(1024)} %param.35) | copy-start | bytes 9220
  211.4 129.3 %all-gather.7.cloned.1.call-start = ((), (), s32[]{:S(2)}) async-start(), calls=%async_computation.12 | async-start | bytes 4718592 | tf_op jit(solution)/shard_map/all_gather | solution.py:109
  295.6 131.5 %reduce-scatter.13.cloned.1.call-start = ((), (), s32[]{:S(2)}) async-start(), calls=%async_computation.13 | async-start | bytes 4718592 | tf_op jit(solution)/shard_map/reduce_scatter | solution.py:113
  383.6 142.2 %all-gather.9.cloned.1.call-start = ((), (), s32[]{:S(2)}) async-start(), calls=%async_computation.14 | async-start | bytes 4718592 | tf_op jit(solution)/shard_map/all_gather | solution.py:139
  479.7 116.2 %reduce-scatter.15.cloned.1.call-start = ((), (), s32[]{:S(2)}) async-start(), calls=%async_computation.15 | async-start | bytes 4718592 | tf_op jit(solution)/shard_map/reduce_scatter | solution.py:144
  552.4 99.6 %all-gather.11.cloned.1.call-start = ((), (), s32[]{:S(2)}) async-start(), calls=%async_computation.16 | async-start | bytes 4718592 | tf_op jit(solution)/shard_map/all_gather | solution.py:152
  606.9 386.3 %reduce-scatter.17.cloned.1.call-start = ((), (), s32[]{:S(2)}) async-start(), calls=%async_computation.17 | async-start | bytes 4718592 | tf_op jit(solution)/shard_map/reduce_scatter | solution.py:190
  607.1 69.5 %copy-start.45 = (f32[6,512]{1,0:T(8,128)}, f32[6,512]{1,0:T(8,128)S(1)}, u32[]{:S(2)}) copy-start(f32[6,512]{1,0:T(8,128)S(1)} %log_add_fusion.3) | copy-start | bytes 36868
  949.8 163.1 %reduce-scatter.29.cloned.1.call-start = ((), (), s32[]{:S(2)}) async-start(), calls=%async_computation.24 | async-start | bytes 5013504 | tf_op jit(solution)/shard_map/reduce_scatter | solution.py:206
  959.8 192.9 %reduce-scatter.27.cloned.1.call-start = ((), (), s32[]{:S(2)}) async-start(), calls=%async_computation.23 | async-start | bytes 5013504 | tf_op jit(solution)/shard_map/reduce_scatter | solution.py:205
  969.6 245.0 %reduce-scatter.25.cloned.1.call-start = ((), (), s32[]{:S(2)}) async-start(), calls=%async_computation.22 | async-start | bytes 1253376 | tf_op jit(solution)/shard_map/reduce_scatter | solution.py:204
  974.9 300.9 %reduce-scatter.23.cloned.1.call-start = ((), (), s32[]{:S(2)}) async-start(), calls=%async_computation.21 | async-start | bytes 1253376 | tf_op jit(solution)/shard_map/reduce_scatter | solution.py:203
  980.5 356.6 %reduce-scatter.21.cloned.1.call-start = ((), (), s32[]{:S(2)}) async-start(), calls=%async_computation.20 | async-start | bytes 1253376 | tf_op jit(solution)/shard_map/reduce_scatter | solution.py:202
  985.3 412.9 %reduce-scatter.19.cloned.1.call-start = ((), (), s32[]{:S(2)}) async-start(), calls=%async_computation.19 | async-start | bytes 1253376 | tf_op jit(solution)/shard_map/reduce_scatter | solution.py:201
  991.1 534.6 %all-reduce.4.cloned.1.call-start = ((), (), s32[]{:S(2)}) async-start(), calls=%async_computation.18 | async-start | bytes 196608 | tf_op jit(solution)/shard_map/psum | solution.py:212
  999.4 527.9 %copy-start.1 = (bf16[768,1536]{1,0:T(8,128)(2,1)S(1)}, bf16[768,1536]{1,0:T(8,128)(2,1)}, u32[]{:S(2)}) copy-start(bf16[768,1536]{1,0:T(8,128)(2,1)} %param.38) | copy-start | bytes 7077892
  (97 other events, 1400.7 us)
Sparse Core Ops, SparseCore 0:
  16.8 46.0 all-gather.4
  211.5 77.0 reduce-scatter.10
  295.7 44.9 all-gather.6
  383.7 43.3 reduce-scatter.12
  479.9 45.9 all-gather.8
  552.5 43.3 reduce-scatter.14
  607.0 44.9 all-gather.10
  949.9 43.3 reduce-scatter.16
  997.7 75.5 reduce-scatter.28
  1078.0 74.6 reduce-scatter.26
  1157.0 57.6 reduce-scatter.24
  1218.7 57.0 reduce-scatter.22
  1280.0 57.0 reduce-scatter.20
  1341.1 57.0 reduce-scatter.18
  1404.2 121.4 all-reduce.3
where the time goes:
time: 1540 us
  waiting for transfers between devices  760 us (49%)
  matrix products  424 us (28%)
  other arithmetic  173 us (11%)
  blocking collectives  141 us (9%)
  between operations  20.3 us (1%)
  local copies, waits for them, and re-layouts  15.7 us (1%)
    psum x1, waiting for transfers between devices, per_device(): lax.psum((d_table, d_gain_one, d_shift_one, d_gain_two, d_shift_two, d_bi...  127 us
    psum x2, blocking collectives, per_device(): lax.psum((jnp.sum(counted * entropy), jnp.sum(counted)), ('rows', 'heads'))  87 us
    convert_element_type x4, other arithmetic, per_device(): d_scores = (probs * (d_probs - row_dot)).astype(bf16)  86.7 us
    reduce_scatter x1, waiting for transfers between devices, per_device(): lax.psum_scatter(jnp.dot(attn_heads, w_out, preferred_element_type=f32),...  77.2 us
    dot_general x4, matrix products, per_device(): jnp.einsum('qhd,khd->hqk', grad_block, value3, preferred_element_type=f32)  68.1 us
    reduce_scatter x1, waiting for transfers between devices, per_device(): lax.psum_scatter(d_w_out, 'rows', scatter_dimension=1, tiled=True)  61.9 us
    reduce_scatter x1, waiting for transfers between devices, per_device(): lax.psum_scatter(d_w_key, 'rows', scatter_dimension=0, tiled=True)  61.3 us
    reduce_scatter x1, waiting for transfers between devices, per_device(): lax.psum_scatter(d_w_value, 'rows', scatter_dimension=0, tiled=True)  61.2 us
  transfers between devices with their start and end apart: 15, of which 14 were waited for; matrix products, arithmetic and copies ran while one was open for 4% of the time, Pallas kernels for 0%

commit v1 on v0

v1 whole, which is shorter than its diff:
```python
import functools

import jax
import jax.numpy as jnp
from jax import lax
from jax.experimental import pallas as pl
from jax.experimental.pallas import tpu as pltpu
from jax.sharding import PartitionSpec as P

HEAD_DIM = 64
PAIR = 2 * HEAD_DIM
NEG = -1e30
SCALE = HEAD_DIM ** (-0.5)
entropy_weight = 16.0
f32 = jnp.float32
bf16 = jnp.bfloat16
NT = (((1,), (1,)), ((), ()))
TN = (((0,), (0,)), ((), ()))
NN = (((1,), (0,)), ((), ()))
VMEM_LIMIT = 56 << 20


def mm(a, b, dims=NN):
    return lax.dot_general(a, b, dims, preferred_element_type=f32)


def layer_norm(values, gain, shift):
    centre = values - jnp.mean(values, axis=-1, keepdims=True)
    spread = jnp.mean(centre * centre, axis=-1, keepdims=True)
    return centre * lax.rsqrt(spread + 1e-05) * gain + shift


def gelu_exact(values):
    return jax.nn.gelu(values, approximate=False)


def split3(x):
    hi = x.astype(bf16).astype(f32)
    mid = (x - hi).astype(bf16).astype(f32)
    return hi, mid, x - hi - mid


def pair_masks():
    lane = lax.broadcasted_iota(jnp.int32, (1, PAIR), 1)
    return lane, (lane < HEAD_DIM, lane >= HEAD_DIM), (HEAD_DIM, 0)


def own_part(h):
    return slice(0, HEAD_DIM) if h == 0 else slice(HEAD_DIM, PAIR)


def key_bias(meta, keys):
    kpos = meta[0] + lax.broadcasted_iota(jnp.int32, (keys, 1), 0)
    return jnp.where(kpos < meta[1], 0.0, NEG)


def attn_fwd_kernel(first, qb, kc, meta, q_ref, k_ref, v_ref, *refs):
    if first:
        acc_ref, ml_ref, st_sc, p_sc = refs
    else:
        acc_in, ml_in, o_ref, e_ref, acc_sc, e_sc, st_sc, p_sc = refs
    rows = q_ref.shape[0]
    keys = k_ref.shape[0]
    lane, inside, free = pair_masks()
    bias = key_bias(meta, keys)
    q32 = q_ref[...].astype(f32) * SCALE
    k32 = k_ref[...].astype(f32)
    v32 = v_ref[...].astype(f32)
    qx = [jnp.where(inside[h], q32, jnp.where(lane == free[h], 1.0, 0.0)).astype(bf16) for h in range(2)]
    kx = [jnp.where(inside[h], k32, bias).astype(bf16) for h in range(2)]
    vx = [jnp.where(inside[h], v32, 1.0).astype(bf16) for h in range(2)]
    units = [(h, b) for h in range(2) for b in range(rows // qb)]
    chunks = [slice(c * kc, (c + 1) * kc) for c in range(keys // kc)]
    m_prev = None
    for u in range(len(units) + 1):
        slot, prev = u % 2, (u - 1) % 2
        if u < len(units):
            h, b = units[u]
            cols = slice(b * qb, (b + 1) * qb)
        m8 = None
        for ch in chunks:
            if u < len(units):
                st = mm(kx[h][ch], qx[h][cols], NT)
                st_sc[slot, ch, :] = st
                top = jnp.max(st.reshape(kc // 8, 8, qb), axis=0)
                m8 = top if m8 is None else jnp.maximum(m8, top)
            if u > 0:
                p_sc[prev, ch, :] = jnp.exp(st_sc[prev, ch, :] - m_prev).astype(bf16)
        if u > 0:
            hp, bp = units[u - 1]
            pc = slice(bp * qb, (bp + 1) * qb)
            ot = mm(vx[hp], p_sc[prev], TN)
            fe = free[hp]
            own = own_part(hp)
            total = ot[fe : fe + 1]
            num = ot[own]
            if first:
                acc_ref[own, pc] = num
                ml_ref[hp : hp + 1, pc] = m_prev
                ml_ref[2 + hp : 3 + hp, pc] = total
            else:
                alpha = jnp.exp(ml_in[hp : hp + 1, pc] - m_prev)
                total = total + alpha * ml_in[2 + hp : 3 + hp, pc]
                num = num + alpha * acc_in[own, pc]
                acc_sc[own, pc] = num / total
                hi, mid, lo = split3(m_prev + jnp.log(total))
                row = lax.broadcasted_iota(jnp.int32, (HEAD_DIM, 1), 0)
                e_sc[fe : fe + HEAD_DIM, pc] = jnp.where(
                    row == 0, 1.0, jnp.where(row == 1, -hi, jnp.where(row == 2, -mid, jnp.where(row == 3, -lo, 0.0)))
                )
        if u < len(units):
            m_prev = jnp.max(m8, axis=0, keepdims=True)
            if not first:
                m_prev = jnp.maximum(m_prev, ml_in[h : h + 1, cols])
    if not first:
        o_ref[...] = acc_sc[...].T.astype(bf16)
        e_ref[...] = e_sc[...].T.astype(bf16)


def attn_fwd(meta, q, k, v, pairs, state=None, qb=1024, kc=256):
    rows = q[0].shape[0]
    keys = k[0].shape[0]
    width = pairs * PAIR
    first = state is None

    def col(off):
        return lambda i, m: (0, off + i)

    def down(i, m):
        return (i, 0)

    in_specs = [
        pl.BlockSpec((rows, PAIR), col(q[1])),
        pl.BlockSpec((keys, PAIR), col(k[1])),
        pl.BlockSpec((keys, PAIR), col(v[1])),
    ]
    scratch = [pltpu.VMEM((2, keys, qb), f32), pltpu.VMEM((2, keys, qb), bf16)]
    args = (q[0], k[0], v[0])
    if first:
        out_shape = (jax.ShapeDtypeStruct((width, rows), f32), jax.ShapeDtypeStruct((8 * pairs, rows), f32))
        out_specs = (pl.BlockSpec((PAIR, rows), down), pl.BlockSpec((8, rows), down))
    else:
        in_specs += [pl.BlockSpec((PAIR, rows), down), pl.BlockSpec((8, rows), down)]
        out_shape = (jax.ShapeDtypeStruct((rows, width), bf16), jax.ShapeDtypeStruct((rows, width), bf16))
        out_specs = (pl.BlockSpec((rows, PAIR), col(0)), pl.BlockSpec((rows, PAIR), col(0)))
        scratch = [pltpu.VMEM((PAIR, rows), f32), pltpu.VMEM((PAIR, rows), f32)] + scratch
        args = args + tuple(state)
    return pl.pallas_call(
        functools.partial(attn_fwd_kernel, first, qb, kc),
        grid_spec=pltpu.PrefetchScalarGridSpec(
            num_scalar_prefetch=1, grid=(pairs,), in_specs=in_specs, out_specs=out_specs, scratch_shapes=scratch
        ),
        out_shape=out_shape,
        compiler_params=pltpu.CompilerParams(vmem_limit_bytes=VMEM_LIMIT),
        cost_estimate=pl.CostEstimate(flops=16 * rows * keys * width, transcendentals=0, bytes_accessed=8 * rows * width),
        name="attn_fwd_first" if first else "attn_fwd_second",
    )(meta, *args)


def attn_bwd_kernel(first, qb, kc, meta, q_ref, e_ref, o_ref, do_ref, k_ref, v_ref, *refs):
    if first:
        dq_ref, dk_ref, dv_ref, dk_sc, dv_sc, s_sc, dp_sc, p_sc, ds_sc = refs
    else:
        dq_in, dq_ref, dk_ref, dv_ref, dk_sc, dv_sc, s_sc, dp_sc, p_sc, ds_sc = refs
    rows = q_ref.shape[0]
    keys = k_ref.shape[0]
    lane, inside, free = pair_masks()
    bias = key_bias(meta, keys)
    k32 = k_ref[...].astype(f32)
    v32 = v_ref[...].astype(f32)
    kx = [jnp.where(inside[h], k32, jnp.where(lane == free[h], bias, 1.0)).astype(bf16) for h in range(2)]
    vx = [jnp.where(inside[h], v32, 1.0).astype(bf16) for h in range(2)]
    units = [(b, h) for b in range(rows // qb) for h in range(2)]
    chunks = [slice(c * kc, (c + 1) * kc) for c in range(keys // kc)]
    prep = None
    dq0 = None
    for u in range(len(units) + 1):
        before = prep
        slot, prev = u % 2, (u - 1) % 2
        if u < len(units):
            b, h = units[u]
            rs = slice(b * qb, (b + 1) * qb)
            fe = free[h]
            if h == 0:
                q32 = q_ref[rs].astype(f32) * SCALE
                do32 = do_ref[rs].astype(f32)
                e32 = e_ref[rs].astype(f32)
                prod = do32 * o_ref[rs].astype(f32)
            hi, mid, lo = split3(jnp.sum(jnp.where(inside[h], prod, 0.0), axis=1, keepdims=True))
            dext = jnp.where(lane == fe, -hi, jnp.where(lane == fe + 1, -mid, jnp.where(lane == fe + 2, -lo, 0.0)))
            qx = jnp.where(inside[h], q32, e32).astype(bf16)
            dox = jnp.where(inside[h], do32, dext).astype(bf16)
            prep = (qx, dox)
        for ch in chunks:
            if u < len(units):
                s_sc[slot, :, ch] = mm(qx, kx[h][ch], NT)
                dp_sc[slot, :, ch] = mm(dox, vx[h][ch], NT)
            if u > 0:
                p = jnp.exp(s_sc[prev, :, ch])
                p_sc[prev, :, ch] = p.astype(bf16)
                ds_sc[prev, :, ch] = (p * dp_sc[prev, :, ch]).astype(bf16)
        if u > 0:
            bp, hp = units[u - 1]
            rp = slice(bp * qb, (bp + 1) * qb)
            qxp, doxp = before
            dvt = mm(doxp, p_sc[prev], TN)
            dkt = mm(qxp, ds_sc[prev], TN)
            dqh = mm(ds_sc[prev], kx[hp], NN)
            own = own_part(hp)
            if bp == 0:
                dv_sc[own] = dvt[own]
                dk_sc[own] = dkt[own]
            else:
                dv_sc[own] += dvt[own]
                dk_sc[own] += dkt[own]
            if hp == 0:
                dq0 = dqh
            else:
                dq = jnp.where(lane < HEAD_DIM, dq0, dqh) * SCALE
                if first:
                    dq_ref[rp] = dq
                else:
                    dq_ref[rp] = (dq + dq_in[rp]).astype(bf16)
    dk_ref[...] = dk_sc[...].T.astype(bf16)
    dv_ref[...] = dv_sc[...].T.astype(bf16)


def attn_bwd(meta, q, e, o, do, k, v, pairs, dq_prev=None, qb=256, kc=256):
    rows = q[0].shape[0]
    keys = k[0].shape[0]
    width = pairs * PAIR
    first = dq_prev is None

    def col(off):
        return lambda i, m: (0, off + i)

    in_specs = [pl.BlockSpec((rows, PAIR), col(off)) for _, off in (q, e, o, do)]
    in_specs += [pl.BlockSpec((keys, PAIR), col(off)) for _, off in (k, v)]
    args = (q[0], e[0], o[0], do[0], k[0], v[0])
    rspec = pl.BlockSpec((rows, PAIR), col(0))
    kspec = pl.BlockSpec((keys, PAIR), col(0))
    if not first:
        in_specs.append(rspec)
        args = args + (dq_prev,)
    return pl.pallas_call(
        functools.partial(attn_bwd_kernel, first, qb, kc),
        grid_spec=pltpu.PrefetchScalarGridSpec(
            num_scalar_prefetch=1,
            grid=(pairs,),
            in_specs=in_specs,
            out_specs=(rspec, kspec, kspec),
            scratch_shapes=[pltpu.VMEM((PAIR, keys), f32)] * 2
            + [pltpu.VMEM((2, qb, keys), f32)] * 2
            + [pltpu.VMEM((2, qb, keys), bf16)] * 2,
        ),
        out_shape=(
            jax.ShapeDtypeStruct((rows, width), f32 if first else bf16),
            jax.ShapeDtypeStruct((keys, width), bf16),
            jax.ShapeDtypeStruct((keys, width), bf16),
        ),
        compiler_params=pltpu.CompilerParams(vmem_limit_bytes=VMEM_LIMIT),
        cost_estimate=pl.CostEstimate(flops=40 * rows * keys * width, transcendentals=0, bytes_accessed=16 * rows * width),
        name="attn_bwd_first" if first else "attn_bwd_second",
    )(meta, *args)


class Net:
    def __init__(self, n_rows):
        self.n_rows = n_rows
        self.bits = n_rows.bit_length() - 1
        self.row = lax.axis_index("rows")

    def cross(self, x):
        return lax.ppermute(x, "heads", [(0, 1), (1, 0)])

    def flip(self, x, bit):
        return lax.ppermute(x, "rows", [(i, i ^ (1 << bit)) for i in range(self.n_rows)])

    def bit(self, b):
        return (self.row >> b) & 1

    def fetch(self, own):
        part = own.shape[0] // 2
        mine = self.bit(0) * part
        got = self.cross(lax.dynamic_slice_in_dim(own, mine, part, 0))
        passed = self.flip(got, 0)
        full = jnp.zeros(own.shape, own.dtype)
        full = lax.dynamic_update_slice_in_dim(full, got, mine, 0)
        return lax.dynamic_update_slice_in_dim(full, passed, part - mine, 0)

    def all_sum(self, whole, own, other):
        n_whole = whole.shape[0]
        packed = jnp.concatenate([whole, own, other], axis=0)
        for b in range(self.bits):
            packed = packed + self.flip(packed, b)
        n_own = own.shape[0]
        send = jnp.concatenate([packed[:n_whole], packed[n_whole + n_own :]], axis=0)
        return packed[: n_whole + n_own] + self.cross(send)

    def scatter_sum(self, own, other, order):
        rows, cols = own.shape
        piece = rows // self.n_rows
        parts = [own.reshape(self.n_rows, piece, cols), other.reshape(self.n_rows, piece, cols)]
        left = list(range(self.bits))
        for step in order:
            if step == "x":
                mine, theirs = parts
                parts = [mine.astype(f32) + self.cross(theirs.astype(bf16)).astype(f32)]
                continue
            low = 1 << left.index(step)
            left.remove(step)
            at = self.bit(step)
            views = [p.reshape(p.shape[0] // (2 * low), 2, low, piece, cols) for p in parts]
            keep = [lax.dynamic_index_in_dim(v, at, 1, keepdims=False) for v in views]
            send = [lax.dynamic_index_in_dim(v, 1 - at, 1, keepdims=False).astype(bf16) for v in views]
            got = self.flip(jnp.concatenate(send, axis=-1), step) if len(send) > 1 else self.flip(send[0], step)
            got = [got[..., i * cols : (i + 1) * cols] for i in range(len(send))]
            parts = [
                (k.astype(f32) + g.astype(f32)).reshape(k.shape[0] * k.shape[1], piece, cols) for k, g in zip(keep, got)
            ]
        return parts[0].reshape(piece, cols)


def per_device(
    n_rows,
    tokens,
    crop_lengths,
    lead_index,
    valid_mask,
    lead_table,
    ln1_gain,
    ln1_shift,
    w_query,
    w_key,
    w_value,
    b_query,
    b_value,
    w_out,
    b_out,
    ln2_gain,
    ln2_shift,
    w_up,
    b_up,
    w_down,
    b_down,
    w_gater,
    cotangent,
):
    net = Net(n_rows)
    own_rows, width = tokens.shape
    half = lax.axis_index("heads")
    length = crop_lengths[0]
    hw = w_query.shape[1]
    pairs = hw // PAIR
    own_start = half * own_rows
    meta_own = jnp.stack([own_start, length])
    meta_oth = jnp.stack([own_rows - own_start, length])

    positions = own_start + jnp.arange(own_rows, dtype=jnp.int32)
    counted = ((positions < length) & (valid_mask == 1)).astype(f32)
    count = jnp.full((8, 128), jnp.sum(counted), f32)
    for b in range(net.bits):
        count = count + net.flip(count, b)
    count_total = (count + net.cross(count))[0, 0]

    qkv_w = jnp.concatenate([w_query, w_key, w_value], axis=1)
    bias_own = jnp.concatenate([b_query, b_value, b_up]).reshape(1, -1)
    bias_oth = net.cross(jnp.broadcast_to(bias_own, (16, bias_own.shape[1])))[:1]
    qkv_w2 = net.fetch(qkv_w)
    tokens_in, qkv_w2 = lax.optimization_barrier((tokens, qkv_w2))
    tokens_oth = net.cross(tokens_in)
    w_out_in, w_up_in, w_down_in, tokens_oth = lax.optimization_barrier((w_out, w_up, w_down, tokens_oth))
    w_out2 = net.fetch(w_out_in)
    w_up_in, w_out2 = lax.optimization_barrier((w_up_in, w_out2))
    w_up2 = net.fetch(w_up_in)
    w_down_in, w_up2 = lax.optimization_barrier((w_down_in, w_up2))
    w_down2 = net.fetch(w_down_in)

    def qkv_bias(b):
        b = b.astype(f32)
        return jnp.concatenate([b[:, :hw], jnp.zeros((1, hw), f32), b[:, hw : 2 * hw]], axis=1)

    qkv_b, qkv_b2 = qkv_bias(bias_own), qkv_bias(bias_oth)
    up_b, up_b2 = bias_own[:, 2 * hw :].astype(f32), bias_oth[:, 2 * hw :].astype(f32)

    picked = jnp.arange(lead_table.shape[0], dtype=jnp.int32) == lead_index[0]
    embedding = jnp.sum(jnp.where(picked[:, None], lead_table, 0.0), axis=0)
    x_zero = tokens.astype(f32) + embedding
    normed = layer_norm(x_zero, ln1_gain, ln1_shift).astype(bf16)
    qkv = [(mm(normed, qkv_w) + qkv_b).astype(bf16)]
    state = [attn_fwd(meta_own, (qkv[0], 0), (qkv[0], pairs), (qkv[0], 2 * pairs), pairs)]
    qkv.append((mm(normed, qkv_w2) + qkv_b2).astype(bf16))
    state.append(attn_fwd(meta_own, (qkv[1], 0), (qkv[1], pairs), (qkv[1], 2 * pairs), pairs))
    normed_oth = layer_norm(tokens_oth.astype(f32) + embedding, ln1_gain, ln1_shift).astype(bf16)
    kv_oth = [
        (mm(normed_oth, w[:, hw:]) + b[:, hw:]).astype(bf16) for w, b in ((qkv_w, qkv_b), (qkv_w2, qkv_b2))
    ]
    attn, ext = [], []
    for i in range(2):
        o, e = attn_fwd(meta_oth, (qkv[i], 0), (kv_oth[i], 0), (kv_oth[i], pairs), pairs, state[i])
        attn.append(o)
        ext.append(e)

    hidden_one = x_zero + (mm(attn[0], w_out) + mm(attn[1], w_out2) + b_out)
    normed_two = layer_norm(hidden_one, ln2_gain, ln2_shift).astype(bf16)
    ups, downs, up_bs = (w_up, w_up2), (w_down, w_down2), (up_b, up_b2)
    pre = [mm(normed_two, ups[i]) + up_bs[i] for i in range(2)]
    act = [gelu_exact(p).astype(bf16) for p in pre]
    output = hidden_one + (mm(act[0], w_down) + mm(act[1], w_down2) + b_down)

    logits = jnp.einsum("dc,td->ct", w_gater, output, precision=lax.Precision.HIGHEST)
    log_probs = jax.nn.log_softmax(logits, axis=0)
    gate_probs = jnp.exp(log_probs)
    entropy = -jnp.sum(gate_probs * log_probs, axis=0)
    entropy_sum = jnp.sum(counted * entropy)
    mean_logit = jnp.sum(gate_probs * logits, axis=0)
    d_logits = entropy_weight / count_total * counted * (-gate_probs * (logits - mean_logit))
    d_output = cotangent.astype(f32) + jnp.einsum("dc,ct->td", w_gater, d_logits, precision=lax.Precision.HIGHEST)
    d_gater = jnp.einsum("td,ct->cd", output, d_logits, precision=lax.Precision.HIGHEST)
    d_branch = d_output.astype(bf16)
    d_bias_down = jnp.sum(d_branch.astype(f32), axis=0)

    d_down = [mm(d_branch, a, TN).astype(bf16) for a in act]
    g_down = net.scatter_sum(d_down[0], d_down[1], [0, 1, 2, 3, "x"] + list(range(4, net.bits)))
    d_pre = []
    for i in range(2):
        gelu_back = jax.vjp(gelu_exact, pre[i])[1]
        d_pre.append(gelu_back(mm(d_branch, downs[i], NT))[0].astype(bf16))
    d_up = [mm(normed_two, d, TN).astype(bf16) for d in d_pre]
    g_up = net.scatter_sum(d_up[0], d_up[1], [0, 2, 1, 3, "x"] + list(range(4, net.bits)))
    d_bias_up = [jnp.sum(d.astype(f32), axis=0) for d in d_pre]
    d_normed_two = mm(d_pre[0], w_up, NT) + mm(d_pre[1], w_up2, NT)
    norm_two_back = jax.vjp(layer_norm, hidden_one, ln2_gain, ln2_shift)[1]
    d_hidden_norm, d_gain_two, d_shift_two = norm_two_back(d_normed_two)
    d_hidden = d_output + d_hidden_norm
    d_attn = d_hidden.astype(bf16)
    d_bias_out = jnp.sum(d_attn.astype(f32), axis=0)
    d_heads = [mm(d_attn, w, NT).astype(bf16) for w in (w_out, w_out2)]
    d_wout = [mm(d_attn, a, TN).astype(bf16) for a in attn]
    g_out = net.scatter_sum(d_wout[0], d_wout[1], [0, 1, 2, 3, "x"] + list(range(4, net.bits)))

    whole = jnp.concatenate(
        [d_gater, jnp.stack([d_gain_two, d_shift_two, d_bias_out, d_bias_down, jnp.full((width,), entropy_sum)])]
    )
    sums = net.all_sum(whole, d_bias_up[0].reshape(-1, width), d_bias_up[1].reshape(-1, width))
    d_gater, penalty = sums[:3].T, sums[7, 0] / count_total
    d_gain_two, d_shift_two, d_bias_out, d_bias_down = sums[3], sums[4], sums[5], sums[6]
    d_bias_up_own = sums[8:].reshape(-1)

    dq, dk_oth, dv_oth = [], [], []
    for i in range(2):
        a, b, c = attn_bwd(
            meta_oth, (qkv[i], 0), (ext[i], 0), (attn[i], 0), (d_heads[i], 0), (kv_oth[i], 0), (kv_oth[i], pairs), pairs
        )
        dq.append(a)
        dk_oth.append(b)
        dv_oth.append(c)
    ws = (qkv_w, qkv_w2)
    da_oth = sum(
        mm(dk_oth[i], ws[i][:, hw : 2 * hw], NT) + mm(dv_oth[i], ws[i][:, 2 * hw :], NT) for i in range(2)
    ).astype(bf16)
    da_got = net.cross(da_oth)
    d_qkv = []
    g_qkv = []
    for i in range(2):
        a, b, c = attn_bwd(
            meta_own,
            (qkv[i], 0),
            (ext[i], 0),
            (attn[i], 0),
            (d_heads[i], 0),
            (qkv[i], pairs),
            (qkv[i], 2 * pairs),
            pairs,
            dq[i],
        )
        d_qkv.append((a, b, c))
        g_qkv.append(
            jnp.concatenate(
                [
                    mm(normed, a, TN),
                    mm(normed, b, TN) + mm(normed_oth, dk_oth[i], TN),
                    mm(normed, c, TN) + mm(normed_oth, dv_oth[i], TN),
                ],
                axis=1,
            ).astype(bf16)
        )
    g_qkv_sum = net.scatter_sum(g_qkv[0], g_qkv[1], [0, 1, 2, 3, "x"] + list(range(4, net.bits)))
    da = da_got.astype(f32) + sum(
        mm(d_qkv[i][j], ws[i][:, j * hw : (j + 1) * hw], NT) for i in range(2) for j in range(3)
    )
    norm_one_back = jax.vjp(layer_norm, x_zero, ln1_gain, ln1_shift)[1]
    d_input_norm, d_gain_one, d_shift_one = norm_one_back(da)
    d_tokens = d_hidden + d_input_norm
    d_table = jnp.where(picked[:, None], jnp.sum(d_tokens, axis=0)[None, :], 0.0)
    bias_rows = [
        jnp.concatenate(
            [jnp.sum(d_qkv[i][0].astype(f32), axis=0), jnp.sum(d_qkv[i][2].astype(f32), axis=0) + jnp.sum(dv_oth[i].astype(f32), axis=0)]
        ).reshape(1, -1)
        for i in range(2)
    ]
    late = net.all_sum(
        jnp.concatenate([d_table, d_gain_one.reshape(1, -1), d_shift_one.reshape(1, -1)]), bias_rows[0], bias_rows[1]
    )
    n_lead = lead_table.shape[0]
    return (
        output.astype(bf16),
        penalty,
        d_tokens,
        late[:n_lead],
        late[n_lead],
        late[n_lead + 1],
        g_qkv_sum[:, :hw],
        g_qkv_sum[:, hw : 2 * hw],
        g_qkv_sum[:, 2 * hw :],
        late[n_lead + 2, :hw],
        late[n_lead + 2, hw:],
        g_out.T,
        d_bias_out,
        d_gain_two,
        d_shift_two,
        g_up,
        d_bias_up_own,
        g_down.T,
        d_bias_down,
        d_gater,
    )


def solution(mesh):
    in_specs = (
        P(("rows", "heads"), None),
        P("rows"),
        P("rows"),
        P(("rows", "heads")),
        P(),
        P(),
        P(),
        P(None, "heads"),
        P(None, "heads"),
        P(None, "heads"),
        P("heads"),
        P("heads"),
        P("heads", None),
        P(),
        P(),
        P(),
        P(None, "heads"),
        P("heads"),
        P("heads", None),
        P(),
        P(),
        P(("rows", "heads"), None),
    )
    out_specs = (
        P(("rows", "heads"), None),
        P(),
        P(("rows", "heads"), None),
        P(),
        P(),
        P(),
        P("rows", "heads"),
        P("rows", "heads"),
        P("rows", "heads"),
        P("heads"),
        P("heads"),
        P("heads", "rows"),
        P(),
        P(),
        P(),
        P("rows", "heads"),
        P("heads"),
        P("heads", "rows"),
        P(),
        P(),
    )
    return jax.shard_map(
        functools.partial(per_device, mesh.shape["rows"]),
        mesh=mesh,
        in_specs=in_specs,
        out_specs=out_specs,
        check_vma=False,
    )
```

time: 1540 us -> 651 us (0.42)
  waiting for transfers between devices: 760 us -> 199 us
  matrix products: 424 us -> 168 us
  blocking collectives: 141 us -> 0 us
  other arithmetic: 173 us -> 37 us
  Pallas kernels: 0 us -> 117 us
  starting transfers between devices: 1.28 us -> 54.3 us
  local copies, waits for them, and re-layouts: 15.7 us -> 55.9 us
    reduce_scatter x10 -> x0, waiting for transfers between devices: 451 us -> none  [the longest x1 77.2 us: per_device(): lax.psum_scatter(jnp.dot(attn_heads, w_out, preferred_element_type=f32),...]
    dot_general x43, matrix products: 412 us -> 163 us  [the longest x42 158 us: mm(): return lax.dot_general(a, b, dims, preferred_element_type=f32)]
    ppermute x0 -> x46, waiting for transfers between devices: none -> 199 us  [the longest x32 121 us: flip(): lax.ppermute(x, 'rows', [(i, i ^ 1 << bit) for i in range(self.n_rows)])]
    all_gather x4 -> x0, waiting for transfers between devices: 181 us -> none  [the longest x1 46 us: per_device(): branch_rows = lax.all_gather(d_branch, 'heads', axis=0, tiled=True)]
    psum x3 -> x0, blocking collectives: 141 us -> none  [the longest x2 87 us: per_device(): lax.psum((jnp.sum(counted * entropy), jnp.sum(counted)), ('rows', 'heads'))]
    psum x1 -> x0, waiting for transfers between devices: 127 us -> none  [per_device(): lax.psum((d_table, d_gain_one, d_shift_one, d_gain_two, d_shift_two, d_bi...]
    pallas_call x0 -> x8, Pallas kernels: none -> 117 us  [the longest x4 70 us: attn_bwd(): pl.pallas_call(functools.partial(attn_bwd_kernel, first, qb, kc), grid_sp...]
    convert_element_type x8 -> x6, other arithmetic: 88.6 us -> 2.7 us  [the longest x1 1.83 us: per_device(): layer_norm(tokens_oth.astype(f32) + embedding, ln1_gain, ln1_shift)]
  transfers between devices with their start and end apart: 15 -> 46, of which waited for: 14 -> 27; matrix products, arithmetic and copies ran while one was open for 4% -> 20% of each run, Pallas kernels for 0% -> 4%
where the time goes in v1:
time: 651 us; the launch traced here: 639 us
  waiting for transfers between devices  199 us (31%)
  matrix products  168 us (26%)
  Pallas kernels  117 us (18%)
  local copies, waits for them, and re-layouts  55.9 us (9%)
  starting transfers between devices  54.3 us (8%)
  other arithmetic  37 us (6%)
  between operations  7.48 us (1%)
    dot_general x42, matrix products, mm(): return lax.dot_general(a, b, dims, preferred_element_type=f32)  158 us
    ppermute x32, waiting for transfers between devices, flip(): lax.ppermute(x, 'rows', [(i, i ^ 1 << bit) for i in range(self.n_rows)])  121 us
    ppermute x14, waiting for transfers between devices, cross(): return lax.ppermute(x, 'heads', [(0, 1), (1, 0)])  79 us
    pallas_call x4, Pallas kernels, attn_bwd(): pl.pallas_call(functools.partial(attn_bwd_kernel, first, qb, kc), grid_sp...  70 us
    pallas_call x4, Pallas kernels, attn_fwd(): pl.pallas_call(functools.partial(attn_fwd_kernel, first, qb, kc), grid_sp...  47 us
    ppermute x32, starting transfers between devices, flip(): lax.ppermute(x, 'rows', [(i, i ^ 1 << bit) for i in range(self.n_rows)])  38.6 us
    unnamed x220, local copies, waits for them, and re-layouts  28.4 us
    ppermute x14, starting transfers between devices, cross(): return lax.ppermute(x, 'heads', [(0, 1), (1, 0)])  15.8 us
  transfers between devices with their start and end apart: 46, of which 27 were waited for; matrix products, arithmetic and copies ran while one was open for 20% of the time, Pallas kernels for 4%

profile of v1, /device:TPU:8, one launch (start us, length us, event | category | flops | bytes accessed | tf_op | source)
XLA Modules:
  0.0 639.3 jit_solution(11401104689579835734)
XLA Ops:
  9.5 19.9 %collective-permute-done = bf16[384,1152]{1,0:T(8,128)(2,1)S(1)} collective-permute-done((bf16[384,1152]{1,0:T(8,128)(2,1)S(1)}, bf16[384,1152]{1,0:T(8,128)(2,1)S(1)}, u32[]{:S(2)}, u32[]{:S(2)}) %collective-permute-start) | collective-permute-done | bytes 884768 | tf_op jit(solution)/shard_map/ppermute | solution.py:274
  46.8 32.6 %collective-permute-done.2 = bf16[1024,768]{0,1:T(8,128)(2,1)S(1)} collective-permute-done((bf16[1024,768]{0,1:T(8,128)(2,1)}, bf16[1024,768]{0,1:T(8,128)(2,1)S(1)}, u32[]{:S(2)}, u32[]{:S(2)}) %collective-permute-start.2) | collective-permute-done | bytes 1572896 | tf_op jit(solution)/shard_map/ppermute | solution.py:274
  88.3 11.6 %attn_fwd_first.2 = (f32[384,1024]{1,0:T(8,128)}, f32[24,1024]{1,0:T(8,128)}) custom-call(s32[2]{0:T(128)} %get-tuple-element.221.meta, bf16[1024,1152]{1,0:T(8,128)(2,1)} %add_convert_fusion.3.q_ref.k_ref.v_ref, bf16[1024,1152]{1,0:T(8,128)(2,1)} %add_convert_fusion.3.q_ref.k_ref.v_ref, bf16[1024,1152]{1,0:T(8,128)(2,1)} %add_convert_fusion.3.q_ref.k_ref.v_ref), custom_call_target="tpu_custom_call" | custom-call | flops 6442450944 | bytes 3145728 | tf_op jit(solution)/shard_map/attn_fwd_first/pallas_call | solution.py:148
  105.1 11.3 %attn_fwd_first.3 = (f32[384,1024]{1,0:T(8,128)}, f32[24,1024]{1,0:T(8,128)}) custom-call(s32[2]{0:T(128)} %get-tuple-element.221.meta, bf16[1024,1152]{1,0:T(8,128)(2,1)} %add_convert_fusion.2.q_ref.k_ref.v_ref, bf16[1024,1152]{1,0:T(8,128)(2,1)} %add_convert_fusion.2.q_ref.k_ref.v_ref, bf16[1024,1152]{1,0:T(8,128)(2,1)} %add_convert_fusion.2.q_ref.k_ref.v_ref), custom_call_target="tpu_custom_call" | custom-call | flops 6442450944 | bytes 3145728 | tf_op jit(solution)/shard_map/attn_fwd_first/pallas_call | solution.py:148
  119.6 12.1 %attn_fwd_second.2 = (bf16[1024,384]{1,0:T(8,128)(2,1)}, bf16[1024,384]{1,0:T(8,128)(2,1)}) custom-call(s32[2]{0:T(128)} %get-tuple-element.220.meta, bf16[1024,1152]{1,0:T(8,128)(2,1)} %add_convert_fusion.3.q_ref.k_ref.v_ref, bf16[1024,768]{1,0:T(8,128)(2,1)} %add_convert_fusion.7.k_ref.v_ref, bf16[1024,768]{1,0:T(8,128)(2,1)} %add_convert_fusion.7.k_ref.v_ref, ...), custom_call_target="tpu_custom_call" | custom-call | flops 6442450944 | bytes 3145728 | tf_op jit(solution)/shard_map/attn_fwd_second/pallas_call | solution.py:148
  139.6 12.0 %attn_fwd_second.3 = (bf16[1024,384]{1,0:T(8,128)(2,1)}, bf16[1024,384]{1,0:T(8,128)(2,1)}) custom-call(s32[2]{0:T(128)} %get-tuple-element.220.meta, bf16[1024,1152]{1,0:T(8,128)(2,1)} %add_convert_fusion.2.q_ref.k_ref.v_ref, bf16[1024,768]{1,0:T(8,128)(2,1)} %add_convert_fusion.6.k_ref.v_ref, bf16[1024,768]{1,0:T(8,128)(2,1)} %add_convert_fusion.6.k_ref.v_ref, ...), custom_call_target="tpu_custom_call" | custom-call | flops 6442450944 | bytes 3145728 | tf_op jit(solution)/shard_map/attn_fwd_second/pallas_call | solution.py:148
  154.1 11.7 %collective-permute-done.6 = bf16[384,1536]{1,0:T(8,128)(2,1)} collective-permute-done((bf16[384,1536]{1,0:T(8,128)(2,1)}, bf16[384,1536]{1,0:T(8,128)(2,1)}, u32[]{:S(2)}, u32[]{:S(2)}) %collective-permute-start.6) | collective-permute-done | bytes 1179680 | tf_op jit(solution)/shard_map/ppermute | solution.py:274
  170.9 18.9 %multiply_convert_fusion.1 = (bf16[1024,1536]{1,0:T(8,128)(2,1)S(1)}, f32[1024,1536]{1,0:T(8,128)}, f32[1024,1536]{1,0:T(8,128)}) fusion(f32[1536]{0:T(1024)S(1)} %fusion.66, bf16[1024,768]{0,1:T(8,128)(2,1)S(1)} %add_convert_fusion.5, bf16[768,1536]{1,0:T(8,128)(2,1)S(1)} %copy-done), kind=kOutput, calls=%fused_computation.21 | convolution fusion | flops 2519728128 | bytes 19666944 | tf_op jit(solution)/shard_map/dot_general | solution.py:24
  192.5 5.2 collective-permute-done.8
  197.8 18.6 %multiply_convert_fusion = (bf16[1024,1536]{1,0:T(8,128)(2,1)S(1)}, f32[1024,1536]{1,0:T(8,128)}, f32[1024,1536]{1,0:T(8,128)}) fusion(f32[1536]{0:T(1024)S(1)} %copy-done.84, bf16[1024,768]{0,1:T(8,128)(2,1)S(1)} %add_convert_fusion.5, bf16[768,1536]{1,0:T(8,128)(2,1)S(1)} %constant_dynamic-update-slice_fusion.2), kind=kOutput, calls=%fused_computation.8 | convolution fusion | flops 2519728128 | bytes 19666944 | tf_op jit(solution)/shard_map/dot_general | solution.py:24
  258.1 8.7 %convert_reduce_fusion.1 = (f32[1536]{0:T(1024)S(1)}, bf16[1024,1536]{1,0:T(8,128)(2,1)S(1)}) fusion(f32[1024,1536]{1,0:T(8,128)} %get-tuple-element.181, f32[1024,1536]{1,0:T(8,128)} %get-tuple-element.211, f32[1536]{0:T(1024)S(1)} %fusion.66, bf16[1024,768]{0,1:T(8,128)(2,1)S(1)} %get-tuple-element.172, bf16[1536,768]{1,0:T(8,128)(2,1)S(1)} %copy-done.65), kind=kOutput, calls=%fused_computation.5 | convolution fusion | flops 2442656256 | bytes 19673088 | tf_op jit(solution)/shard_map/dot_general | solution.py:24
  269.6 7.9 %convert_reduce_fusion = (f32[1536]{0:T(1024)S(1)}, bf16[1024,1536]{1,0:T(8,128)(2,1)S(1)}) fusion(f32[1024,1536]{1,0:T(8,128)} %get-tuple-element.179, f32[1024,1536]{1,0:T(8,128)} %get-tuple-element.212, f32[1536]{0:T(1024)S(1)} %copy-done.84, bf16[1024,768]{0,1:T(8,128)(2,1)S(1)} %get-tuple-element.172, bf16[1536,768]{1,0:T(8,128)(2,1)S(1)} %copy-done.44), kind=kOutput, calls=%fused_computation.4 | convolution fusion | flops 2442656256 | bytes 19673088 | tf_op jit(solution)/shard_map/dot_general | solution.py:24
  287.3 17.1 %attn_bwd_first.2 = (f32[1024,384]{1,0:T(8,128)}, bf16[1024,384]{1,0:T(8,128)(2,1)}, bf16[1024,384]{1,0:T(8,128)(2,1)}) custom-call(s32[2]{0:T(128)} %get-tuple-element.220.meta, bf16[1024,1152]{1,0:T(8,128)(2,1)} %add_convert_fusion.3.q_ref.k_ref.v_ref, bf16[1024,384]{1,0:T(8,128)(2,1)} %get-tuple-element.66.e_ref, ...), custom_call_target="tpu_custom_call" | custom-call | flops 16106127360 | bytes 6291456 | tf_op jit(solution)/shard_map/attn_bwd_first/pallas_call | solution.py:245
  304.4 17.7 %attn_bwd_second.2 = (bf16[1024,384]{1,0:T(8,128)(2,1)}, bf16[1024,384]{1,0:T(8,128)(2,1)}, bf16[1024,384]{1,0:T(8,128)(2,1)}) custom-call(s32[2]{0:T(128)} %get-tuple-element.221.meta, bf16[1024,1152]{1,0:T(8,128)(2,1)} %add_convert_fusion.3.q_ref.k_ref.v_ref, bf16[1024,384]{1,0:T(8,128)(2,1)} %get-tuple-element.66.e_ref, ...), custom_call_target="tpu_custom_call" | custom-call | flops 16106127360 | bytes 6291456 | tf_op jit(solution)/shard_map/attn_bwd_second/pallas_call | solution.py:245
  332.1 17.6 %attn_bwd_first.3 = (f32[1024,384]{1,0:T(8,128)}, bf16[1024,384]{1,0:T(8,128)(2,1)}, bf16[1024,384]{1,0:T(8,128)(2,1)}) custom-call(s32[2]{0:T(128)} %get-tuple-element.220.meta, bf16[1024,1152]{1,0:T(8,128)(2,1)} %add_convert_fusion.2.q_ref.k_ref.v_ref, bf16[1024,384]{1,0:T(8,128)(2,1)} %get-tuple-element.69.e_ref, ...), custom_call_target="tpu_custom_call" | custom-call | flops 16106127360 | bytes 6291456 | tf_op jit(solution)/shard_map/attn_bwd_first/pallas_call | solution.py:245
  349.6 17.5 %attn_bwd_second.3 = (bf16[1024,384]{1,0:T(8,128)(2,1)}, bf16[1024,384]{1,0:T(8,128)(2,1)}, bf16[1024,384]{1,0:T(8,128)(2,1)}) custom-call(s32[2]{0:T(128)} %get-tuple-element.221.meta, bf16[1024,1152]{1,0:T(8,128)(2,1)} %add_convert_fusion.2.q_ref.k_ref.v_ref, bf16[1024,384]{1,0:T(8,128)(2,1)} %get-tuple-element.69.e_ref, ...), custom_call_target="tpu_custom_call" | custom-call | flops 16106127360 | bytes 6291456 | tf_op jit(solution)/shard_map/attn_bwd_second/pallas_call | solution.py:245
  472.3 7.8 %fusion.77 = (f32[768]{0:T(1024)S(1)}, f32[1024]{0:T(1024)S(1)}, f32[1024,768]{0,1:T(8,128)S(1)}) fusion(f32[768]{0:T(1024)S(1)} %copy-done.75, f32[1024]{0:T(1024)S(1)} %copy-done.69, f32[768]{0:T(1024)S(1)} %copy-done.67, bf16[1024,768]{0,1:T(8,128)(2,1)S(1)} %copy-done.3, bf16[1024,384]{1,0:T(8,128)(2,1)S(1)} %copy-done.28, ...), kind=kOutput, calls=%fused_computation.298 | convolution fusion | flops 614988032 | bytes 23413760 | tf_op jit(solution)/shard_map/dot_general | solution.py:24
  520.1 11.3 %collective-permute-done.27 = bf16[4,1,48,2304]{3,2,0,1:T(8,128)(2,1)S(1)} collective-permute-done((bf16[4,1,48,2304]{3,2,0,1:T(8,128)(2,1)S(1)}, bf16[4,1,48,2304]{3,2,0,1:T(8,128)(2,1)S(1)}, u32[]{:S(2)}, u32[]{:S(2)}) %collective-permute-start.27) | collective-permute-done | bytes 884768 | tf_op jit(solution)/shard_map/ppermute | solution.py:277
  535.5 18.7 %collective-permute-done.28 = bf16[2,1,48,2304]{3,2,0,1:T(8,128)(2,1)S(1)} collective-permute-done((bf16[2,1,48,2304]{3,2,0,1:T(8,128)(2,1)S(1)}, bf16[2,1,48,2304]{3,2,0,1:T(8,128)(2,1)S(1)}, u32[]{:S(2)}, u32[]{:S(2)}) %collective-permute-start.28) | collective-permute-done | bytes 442400 | tf_op jit(solution)/shard_map/ppermute | solution.py:277
  557.9 6.9 %collective-permute-done.29 = bf16[1,1,48,2304]{3,2,1,0:T(8,128)(2,1)S(1)} collective-permute-done((bf16[1,1,48,2304]{3,2,1,0:T(8,128)(2,1)S(1)}, bf16[1,1,48,2304]{3,2,1,0:T(8,128)(2,1)S(1)}, u32[]{:S(2)}, u32[]{:S(2)}) %collective-permute-start.29) | collective-permute-done | bytes 221216 | tf_op jit(solution)/shard_map/ppermute | solution.py:277
  572.5 23.0 %collective-permute-done.42 = bf16[4,1,48,3072]{3,2,0,1:T(8,128)(2,1)S(1)} collective-permute-done((bf16[4,1,48,3072]{3,2,0,1:T(8,128)(2,1)S(1)}, bf16[4,1,48,3072]{3,2,0,1:T(8,128)(2,1)S(1)}, u32[]{:S(2)}, u32[]{:S(2)}) %collective-permute-start.42) | collective-permute-done | bytes 1179680 | tf_op jit(solution)/shard_map/ppermute | solution.py:277
  597.3 8.5 %collective-permute-done.38 = bf16[2,1,48,3072]{3,2,1,0:T(8,128)(2,1)S(1)} collective-permute-done((bf16[2,1,48,3072]{3,2,1,0:T(8,128)(2,1)S(1)}, bf16[2,1,48,3072]{3,2,1,0:T(8,128)(2,1)S(1)}, u32[]{:S(2)}, u32[]{:S(2)}) %collective-permute-start.38) | collective-permute-done | bytes 589856 | tf_op jit(solution)/shard_map/ppermute | solution.py:277
  610.5 14.3 %collective-permute-done.39 = bf16[1,1,48,3072]{3,2,1,0:T(8,128)(2,1)S(1)} collective-permute-done((bf16[1,1,48,3072]{3,2,1,0:T(8,128)(2,1)S(1)}, bf16[1,1,48,3072]{3,2,1,0:T(8,128)(2,1)S(1)}, u32[]{:S(2)}, u32[]{:S(2)}) %collective-permute-start.39) | collective-permute-done | bytes 294944 | tf_op jit(solution)/shard_map/ppermute | solution.py:277
  625.5 5.6 collective-permute-done.44
  (530 shorter events, 295.1 us)
Async XLA Ops:
  7.9 21.5 %collective-permute-start = (bf16[384,1152]{1,0:T(8,128)(2,1)S(1)}, bf16[384,1152]{1,0:T(8,128)(2,1)S(1)}, u32[]{:S(2)}, u32[]{:S(2)}) collective-permute-start(bf16[384,1152]{1,0:T(8,128)(2,1)S(1)} %constant_dynamic-slice_fusion.3), channel_id=1, source_target_pairs={{0,1},{1,0},{2,3},{3,2},{4,5},{5,4},{6,7},{7,6},{8,9},{9,8},{10,11... | collective-permute-start | bytes 2654216 | tf_op jit(solution)/shard_map/ppermute | solution.py:274
  29.4 8.6 %collective-permute-start.1 = (bf16[384,1152]{1,0:T(8,128)(2,1)S(1)}, bf16[384,1152]{1,0:T(8,128)(2,1)}, u32[]{:S(2)}, u32[]{:S(2)}) collective-permute-start(bf16[384,1152]{1,0:T(8,128)(2,1)S(1)} %collective-permute-done), channel_id=1, source_target_pairs={{0,2},{2,0},{4,6},{6,4},{8,10},{10,8},{12,14},{14,12},{16,18},{18,... | collective-permute-start | bytes 2654216 | tf_op jit(solution)/shard_map/ppermute | solution.py:277
  30.1 13.9 %collective-permute-start.3 = (bf16[16,2304]{1,0:T(8,128)(2,1)S(1)}, bf16[16,2304]{1,0:T(8,128)(2,1)}, u32[]{:S(2)}, u32[]{:S(2)}) collective-permute-start(bf16[16,2304]{1,0:T(8,128)(2,1)S(1)} %broadcast_in_dim.48), channel_id=1, source_target_pairs={{0,1},{1,0},{2,3},{3,2},{4,5},{5,4},{6,7},{7,6},{8,9},{9,8},{10,11... | collective-permute-start | bytes 221192 | tf_op jit(solution)/shard_map/ppermute | solution.py:274
  42.7 36.7 %collective-permute-start.2 = (bf16[1024,768]{0,1:T(8,128)(2,1)}, bf16[1024,768]{0,1:T(8,128)(2,1)S(1)}, u32[]{:S(2)}, u32[]{:S(2)}) collective-permute-start(bf16[1024,768]{0,1:T(8,128)(2,1)} %copy.112), channel_id=1, source_target_pairs={{0,1},{1,0},{2,3},{3,2},{4,5},{5,4},{6,7},{7,6},{8,9},{9,8},{10,11... | collective-permute-start | bytes 4718600 | tf_op jit(solution)/shard_map/ppermute | solution.py:274
  116.4 15.4 %collective-permute-start.4 = (bf16[192,768]{1,0:T(8,128)(2,1)S(1)}, bf16[192,768]{1,0:T(8,128)(2,1)S(1)}, u32[]{:S(2)}, u32[]{:S(2)}) collective-permute-start(bf16[192,768]{1,0:T(8,128)(2,1)S(1)} %constant_dynamic-slice_fusion.2), channel_id=1, source_target_pairs={{0,1},{1,0},{2,3},{3,2},{4,5},{5,4},{6,7},{7,6},{8,9},{9,8},{10,11... | collective-permute-start | bytes 884744 | tf_op jit(solution)/shard_map/ppermute | solution.py:274
  137.1 28.7 %collective-permute-start.6 = (bf16[384,1536]{1,0:T(8,128)(2,1)}, bf16[384,1536]{1,0:T(8,128)(2,1)}, u32[]{:S(2)}, u32[]{:S(2)}) collective-permute-start(bf16[384,1536]{1,0:T(8,128)(2,1)} %constant_dynamic-slice_fusion.1), channel_id=1, source_target_pairs={{0,1},{1,0},{2,3},{3,2},{4,5},{5,4},{6,7},{7,6},{8,9},{9,8},{10,11... | collective-permute-start | bytes 3538952 | tf_op jit(solution)/shard_map/ppermute | solution.py:274
  169.3 28.4 %collective-permute-start.8 = (bf16[768,768]{1,0:T(8,128)(2,1)S(1)}, bf16[768,768]{1,0:T(8,128)(2,1)S(1)}, u32[]{:S(2)}, u32[]{:S(2)}) collective-permute-start(bf16[768,768]{1,0:T(8,128)(2,1)S(1)} %constant_dynamic-slice_fusion), channel_id=1, source_target_pairs={{0,1},{1,0},{2,3},{3,2},{4,5},{5,4},{6,7},{7,6},{8,9},{9,8},{10,11... | collective-permute-start | bytes 3538952 | tf_op jit(solution)/shard_map/ppermute | solution.py:274
  197.8 19.0 %collective-permute-start.9 = (bf16[768,768]{1,0:T(8,128)(2,1)S(1)}, bf16[768,768]{1,0:T(8,128)(2,1)S(1)}, u32[]{:S(2)}, u32[]{:S(2)}) collective-permute-start(bf16[768,768]{1,0:T(8,128)(2,1)S(1)} %collective-permute-done.8), channel_id=1, source_target_pairs={{0,2},{2,0},{4,6},{6,4},{8,10},{10,8},{12,14},{14,12},{16,18},{18,... | collective-permute-start | bytes 3538952 | tf_op jit(solution)/shard_map/ppermute | solution.py:277
  408.4 25.6 %collective-permute-start.15 = (f32[12,768]{1,0:T(8,128)S(1)}, f32[12,768]{1,0:T(8,128)S(1)}, u32[]{:S(2)}, u32[]{:S(2)}) collective-permute-start(f32[12,768]{1,0:T(8,128)S(1)} %concatenate.147), channel_id=1, source_target_pairs={{0,2},{2,0},{4,6},{6,4},{8,10},{10,8},{12,14},{14,12},{16,18},{18,... | collective-permute-start | bytes 110600 | tf_op jit(solution)/shard_map/ppermute | solution.py:277
  416.4 55.8 %collective-permute-start.20 = (bf16[1024,768]{0,1:T(8,128)(2,1)}, bf16[1024,768]{0,1:T(8,128)(2,1)}, u32[]{:S(2)}, u32[]{:S(2)}) collective-permute-start(bf16[1024,768]{0,1:T(8,128)(2,1)} %add_convert_fusion.4), channel_id=1, source_target_pairs={{0,1},{1,0},{2,3},{3,2},{4,5},{5,4},{6,7},{7,6},{8,9},{9,8},{10,11... | collective-permute-start | bytes 4718600 | tf_op jit(solution)/shard_map/ppermute | solution.py:274
  426.2 65.8 %collective-permute-start.26 = (bf16[8,1,48,2304]{3,2,0,1:T(8,128)(2,1)}, bf16[8,1,48,2304]{3,2,0,1:T(8,128)(2,1)}, u32[]{:S(2)}, u32[]{:S(2)}) collective-permute-start(bf16[8,1,48,2304]{3,2,0,1:T(8,128)(2,1)} %pad_maximum_fusion.4), channel_id=1, source_target_pairs={{0,2},{2,0},{4,6},{6,4},{8,10},{10,8},{12,14},{14,12},{16,18},{18,... | collective-permute-start | bytes 5308424 | tf_op jit(solution)/shard_map/ppermute | solution.py:277
  426.9 22.1 %collective-permute-start.31 = (bf16[8,1,48,768]{3,2,0,1:T(8,128)(2,1)S(1)}, bf16[8,1,48,768]{3,2,0,1:T(8,128)(2,1)S(1)}, u32[]{:S(2)}, u32[]{:S(2)}) collective-permute-start(bf16[8,1,48,768]{3,2,0,1:T(8,128)(2,1)S(1)} %pad_maximum_fusion.8), channel_id=1, source_target_pairs={{0,2},{2,0},{4,6},{6,4},{8,10},{10,8},{12,14},{14,12},{16,18},{18,... | collective-permute-start | bytes 1769480 | tf_op jit(solution)/shard_map/ppermute | solution.py:277
  430.6 85.2 %collective-permute-start.36 = (bf16[8,1,48,3072]{3,2,0,1:T(8,128)(2,1)}, bf16[8,1,48,3072]{3,2,0,1:T(8,128)(2,1)}, u32[]{:S(2)}, u32[]{:S(2)}) collective-permute-start(bf16[8,1,48,3072]{3,2,0,1:T(8,128)(2,1)} %pad_maximum_fusion), channel_id=1, source_target_pairs={{0,2},{2,0},{4,6},{6,4},{8,10},{10,8},{12,14},{14,12},{16,18},{18,... | collective-permute-start | bytes 7077896 | tf_op jit(solution)/shard_map/ppermute | solution.py:277
  454.4 78.6 %collective-permute-start.41 = (bf16[8,1,48,3072]{3,2,0,1:T(8,128)(2,1)}, bf16[8,1,48,3072]{3,2,0,1:T(8,128)(2,1)}, u32[]{:S(2)}, u32[]{:S(2)}) collective-permute-start(bf16[8,1,48,3072]{3,2,0,1:T(8,128)(2,1)} %pad_maximum_fusion.1), channel_id=1, source_target_pairs={{0,2},{2,0},{4,6},{6,4},{8,10},{10,8},{12,14},{14,12},{16,18},{18,... | collective-permute-start | bytes 7077896 | tf_op jit(solution)/shard_map/ppermute | solution.py:277
  471.6 14.5 %collective-permute-start.35 = (bf16[1,48,384]{2,1,0:T(8,128)(2,1)S(1)}, bf16[1,48,384]{2,1,0:T(8,128)(2,1)S(1)}, u32[]{:S(2)}, u32[]{:S(2)}) collective-permute-start(bf16[1,48,384]{2,1,0:T(8,128)(2,1)S(1)} %fusion.59), channel_id=1, source_target_pairs={{0,1},{1,0},{2,3},{3,2},{4,5},{5,4},{6,7},{7,6},{8,9},{9,8},{10,11... | collective-permute-start | bytes 110600 | tf_op jit(solution)/shard_map/ppermute | solution.py:274
  510.6 20.8 %collective-permute-start.27 = (bf16[4,1,48,2304]{3,2,0,1:T(8,128)(2,1)S(1)}, bf16[4,1,48,2304]{3,2,0,1:T(8,128)(2,1)S(1)}, u32[]{:S(2)}, u32[]{:S(2)}) collective-permute-start(bf16[4,1,48,2304]{3,2,0,1:T(8,128)(2,1)S(1)} %pad_maximum_fusion.7), channel_id=1, source_target_pairs={{0,4},{2,6},{4,0},{6,2},{8,12},{10,14},{12,8},{14,10},{16,20},{18,... | collective-permute-start | bytes 2654216 | tf_op jit(solution)/shard_map/ppermute | solution.py:277
  518.5 51.9 %collective-permute-start.37 = (bf16[2,2,48,3072]{3,2,1,0:T(8,128)(2,1)S(1)}, bf16[2,2,48,3072]{3,2,1,0:T(8,128)(2,1)S(1)}, u32[]{:S(2)}, u32[]{:S(2)}) collective-permute-start(bf16[2,2,48,3072]{3,2,1,0:T(8,128)(2,1)S(1)} %pad_maximum_fusion.5), channel_id=1, source_target_pairs={{0,8},{2,10},{4,12},{6,14},{8,0},{10,2},{12,4},{14,6},{16,24},{18,... | collective-permute-start | bytes 3538952 | tf_op jit(solution)/shard_map/ppermute | solution.py:277
  531.7 22.5 %collective-permute-start.28 = (bf16[2,1,48,2304]{3,2,0,1:T(8,128)(2,1)S(1)}, bf16[2,1,48,2304]{3,2,0,1:T(8,128)(2,1)S(1)}, u32[]{:S(2)}, u32[]{:S(2)}) collective-permute-start(bf16[2,1,48,2304]{3,2,0,1:T(8,128)(2,1)S(1)} %pad_maximum_fusion.11), channel_id=1, source_target_pairs={{0,8},{2,10},{4,12},{6,14},{8,0},{10,2},{12,4},{14,6},{16,24},{18,... | collective-permute-start | bytes 1327112 | tf_op jit(solution)/shard_map/ppermute | solution.py:277
  554.4 10.4 %collective-permute-start.29 = (bf16[1,1,48,2304]{3,2,1,0:T(8,128)(2,1)S(1)}, bf16[1,1,48,2304]{3,2,1,0:T(8,128)(2,1)S(1)}, u32[]{:S(2)}, u32[]{:S(2)}) collective-permute-start(bf16[1,1,48,2304]{3,2,1,0:T(8,128)(2,1)S(1)} %pad_maximum_fusion.15), channel_id=1, source_target_pairs={{0,16},{2,18},{4,20},{6,22},{8,24},{10,26},{12,28},{14,30},{16,0},... | collective-permute-start | bytes 663560 | tf_op jit(solution)/shard_map/ppermute | solution.py:277
  566.5 29.0 %collective-permute-start.42 = (bf16[4,1,48,3072]{3,2,0,1:T(8,128)(2,1)S(1)}, bf16[4,1,48,3072]{3,2,0,1:T(8,128)(2,1)S(1)}, u32[]{:S(2)}, u32[]{:S(2)}) collective-permute-start(bf16[4,1,48,3072]{3,2,0,1:T(8,128)(2,1)S(1)} %pad_maximum_fusion.6), channel_id=1, source_target_pairs={{0,4},{2,6},{4,0},{6,2},{8,12},{10,14},{12,8},{14,10},{16,20},{18,... | collective-permute-start | bytes 3538952 | tf_op jit(solution)/shard_map/ppermute | solution.py:277
  570.9 35.0 %collective-permute-start.38 = (bf16[2,1,48,3072]{3,2,1,0:T(8,128)(2,1)S(1)}, bf16[2,1,48,3072]{3,2,1,0:T(8,128)(2,1)S(1)}, u32[]{:S(2)}, u32[]{:S(2)}) collective-permute-start(bf16[2,1,48,3072]{3,2,1,0:T(8,128)(2,1)S(1)} %pad_maximum_fusion.9), channel_id=1, source_target_pairs={{0,4},{2,6},{4,0},{6,2},{8,12},{10,14},{12,8},{14,10},{16,20},{18,... | collective-permute-start | bytes 1769480 | tf_op jit(solution)/shard_map/ppermute | solution.py:277
  596.0 13.6 %collective-permute-start.43 = (bf16[2,1,48,3072]{3,2,0,1:T(8,128)(2,1)S(1)}, bf16[2,1,48,3072]{3,2,0,1:T(8,128)(2,1)S(1)}, u32[]{:S(2)}, u32[]{:S(2)}) collective-permute-start(bf16[2,1,48,3072]{3,2,0,1:T(8,128)(2,1)S(1)} %pad_maximum_fusion.10), channel_id=1, source_target_pairs={{0,8},{2,10},{4,12},{6,14},{8,0},{10,2},{12,4},{14,6},{16,24},{18,... | collective-permute-start | bytes 1769480 | tf_op jit(solution)/shard_map/ppermute | solution.py:277
  606.1 18.7 %collective-permute-start.39 = (bf16[1,1,48,3072]{3,2,1,0:T(8,128)(2,1)S(1)}, bf16[1,1,48,3072]{3,2,1,0:T(8,128)(2,1)S(1)}, u32[]{:S(2)}, u32[]{:S(2)}) collective-permute-start(bf16[1,1,48,3072]{3,2,1,0:T(8,128)(2,1)S(1)} %pad_maximum_fusion.13), channel_id=1, source_target_pairs={{0,16},{2,18},{4,20},{6,22},{8,24},{10,26},{12,28},{14,30},{16,0},... | collective-permute-start | bytes 884744 | tf_op jit(solution)/shard_map/ppermute | solution.py:277
  609.8 21.3 %collective-permute-start.44 = (bf16[1,1,48,3072]{3,2,1,0:T(8,128)(2,1)S(1)}, bf16[1,1,48,3072]{3,2,1,0:T(8,128)(2,1)S(1)}, u32[]{:S(2)}, u32[]{:S(2)}) collective-permute-start(bf16[1,1,48,3072]{3,2,1,0:T(8,128)(2,1)S(1)} %pad_maximum_fusion.14), channel_id=1, source_target_pairs={{0,16},{2,18},{4,20},{6,22},{8,24},{10,26},{12,28},{14,30},{16,0},... | collective-permute-start | bytes 884744 | tf_op jit(solution)/shard_map/ppermute | solution.py:277
  (128 other events, 1336.8 us)
